TPU v7x, 128 devices: a whole 4x4x4 slice. The times are simulated.
128 devices in a mesh: rows: 8 (over z, core), seq: 16 (over x, y).
Axes of the slice: x: 4, y: 4, z: 4, core: 2. Of those that a mesh axis runs over, the one named last changes fastest.
Arguments:
- queries: bfloat16 [4096, 4096], P('seq'), may hold values from -50 to 50
- keys: bfloat16 [4096, 4096], P('seq'), may hold values from -6 to 6
- values: bfloat16 [4096, 4096], P('seq'), may hold values from -6 to 6
- grad_out: bfloat16 [8, 4096, 4096], P('rows', 'seq'), may hold values from -6 to 6
- table: bfloat16 [33, 4096], replicated, may hold values from -6 to 6
- positions: int32 [8], P('rows'), may hold values from 0 to 4095
- residues: int32 [8], P('rows'), may hold values from 4 to 23
- tiles: int32 [32, 8], replicated, may hold values from 0 to 31, as said below
- counts: int32 [32], replicated, may hold values from 1 to 8, as said below
Outputs:
- grad_queries: bfloat16 [8, 4096, 4096], P('rows', 'seq')
- grad_keys: bfloat16 [8, 4096, 4096], P('rows', 'seq')
- grad_values: bfloat16 [8, 4096, 4096], P('rows', 'seq')
Inputs may be any that keep to these rules, and one draw needn't show every extreme that they name: `tiles`: row i lists key blocks: entry 0 is i itself, the others differ from i and from each other. Only the first counts[i] entries of row i of tiles are used; some query block uses all 8.
All inputs are finite; a program needn't handle non-finite values.
Results may differ from a plain program's by a relative error of at most 0.0085.
Values may be sent and summed in bfloat16 or wider, within the bound.
No kernel may reach another device: no remote copies, remote signals or barrier semaphores. Data moves between devices by JAX's collectives and lax.ppermute only.
A program may use at most 128 MiB of HBM per device.

v0:
```python
import math
import jax
import jax.numpy as jnp
from jax import lax
from jax.sharding import PartitionSpec as P

D_HEAD = 128
BLOCK = 128
TILES = 8


def substitute(grad_out, table, positions, residues, first_token):
    tok_count = grad_out.shape[1]
    spots = (
        jnp.arange(tok_count, dtype=jnp.int32)[None, :] + first_token == positions[:, None]
    ).astype(jnp.float32)
    picks = (jnp.arange(table.shape[0], dtype=jnp.int32)[None, :] == residues[:, None]).astype(
        jnp.bfloat16
    )
    added = jnp.dot(picks, table, preferred_element_type=jnp.float32)
    summed = grad_out.astype(jnp.float32) + spots[:, :, None] * added[:, None, :]
    return summed.astype(jnp.bfloat16)


def log_total(scores):
    row_max = jnp.max(scores, axis=(-2, -1), keepdims=True)
    return row_max + jnp.log(jnp.sum(jnp.exp(scores - row_max), axis=(-2, -1), keepdims=True))


def slot_mask(count_group):
    slots = jnp.arange(TILES, dtype=jnp.int32)
    return (slots[None, :] < count_group[:, None])[:, None, None, :, None]


def tile_onehot(tile_group, block_count):
    return (
        tile_group[:, :, None] == jnp.arange(block_count, dtype=jnp.int32)[None, None, :]
    ).astype(jnp.bfloat16)


def pick_tiles(blocks, onehot):
    return jnp.einsum("gtb,bkhd->gtkhd", onehot, blocks, preferred_element_type=jnp.float32).astype(
        jnp.bfloat16
    )


def add_tiles(total, terms, onehot):
    high_part = terms.astype(jnp.bfloat16)
    low_part = (terms - high_part.astype(jnp.float32)).astype(jnp.bfloat16)
    total = total + jnp.einsum(
        "gtb,rgtkhd->rbkhd", onehot, high_part, preferred_element_type=jnp.float32
    )
    return total + jnp.einsum(
        "gtb,rgtkhd->rbkhd", onehot, low_part, preferred_element_type=jnp.float32
    )


def tile_scores(query_group, key_blocks, onehot, live_slots, softmax_scale):
    key_tiles = pick_tiles(key_blocks, onehot)
    scores = (
        jnp.einsum("gqhd,gtkhd->ghqtk", query_group, key_tiles, preferred_element_type=jnp.float32)
        * softmax_scale
    )
    return (jnp.where(live_slots, scores, -1e30), key_tiles)


def block_stats(query_blocks, key_blocks, tiles, counts, first_block, block_total, softmax_scale):
    group = math.gcd(max(1, 512 // BLOCK), block_total)
    block_count = key_blocks.shape[0]

    def group_stats(group_index):
        offset_at = first_block + group_index * group
        query_group = lax.dynamic_slice_in_dim(query_blocks, offset_at, group, 0)
        tile_group = lax.dynamic_slice_in_dim(tiles, offset_at, group, 0)
        count_group = lax.dynamic_slice_in_dim(counts, offset_at, group, 0)
        scores, unused = tile_scores(
            query_group,
            key_blocks,
            tile_onehot(tile_group, block_count),
            slot_mask(count_group),
            softmax_scale,
        )
        return log_total(scores)[..., 0, 0]

    stacked = lax.map(group_stats, jnp.arange(block_total // group, dtype=jnp.int32))
    return stacked.reshape((block_total,) + stacked.shape[2:])


def per_device(queries, keys, values, grad_out, table, positions, residues, tiles, counts):
    tok_count = queries.shape[0]
    row_devices = lax.axis_size("rows")
    softmax_scale = D_HEAD ** (-0.5)
    query_heads, key_heads, value_heads = (
        lax.all_to_all(queries, "seq", split_axis=1, concat_axis=0, tiled=True),
        lax.all_to_all(keys, "seq", split_axis=1, concat_axis=0, tiled=True),
        lax.all_to_all(values, "seq", split_axis=1, concat_axis=0, tiled=True),
    )
    cotangent = substitute(grad_out, table, positions, residues, lax.axis_index("seq") * tok_count)
    cot_heads = lax.all_to_all(cotangent, "seq", split_axis=2, concat_axis=1, tiled=True)
    seq_len = query_heads.shape[0]
    width_local = query_heads.shape[1]
    heads_local = width_local // D_HEAD
    block_count = seq_len // BLOCK
    row_count = cot_heads.shape[0]
    block_shape = (block_count, BLOCK, heads_local, D_HEAD)
    query_blocks = query_heads.reshape(block_shape)
    key_blocks = key_heads.reshape(block_shape)
    value_blocks = value_heads.reshape(block_shape)
    cot_blocks = cot_heads.reshape((row_count,) + block_shape)
    share_count = block_count // row_devices
    own_stats = block_stats(
        query_blocks,
        key_blocks,
        tiles,
        counts,
        lax.axis_index("rows") * share_count,
        share_count,
        softmax_scale,
    )
    log_totals = lax.all_gather(own_stats, "rows", axis=0, tiled=True)
    group = math.gcd(max(1, 512 // BLOCK), block_count)

    def step(totals, group_index):
        grad_query, grad_keys, grad_values = totals
        offset_at = group_index * group
        query_group = lax.dynamic_slice_in_dim(query_blocks, offset_at, group, 0)
        tile_group = lax.dynamic_slice_in_dim(tiles, offset_at, group, 0)
        count_group = lax.dynamic_slice_in_dim(counts, offset_at, group, 0)
        stats_group = lax.dynamic_slice_in_dim(log_totals, offset_at, group, 0)
        cot_group = lax.dynamic_slice_in_dim(cot_blocks, offset_at, group, 1)
        live_slots = slot_mask(count_group)
        onehot = tile_onehot(tile_group, block_count)
        scores, key_tiles = tile_scores(query_group, key_blocks, onehot, live_slots, softmax_scale)
        value_tiles = pick_tiles(value_blocks, onehot)
        probs = jnp.where(live_slots, jnp.exp(scores - stats_group[:, :, :, None, None]), 0.0)
        probs_bf = probs.astype(jnp.bfloat16)
        grad_probs = jnp.einsum(
            "rgqhd,gtkhd->rghqtk", cot_group, value_tiles, preferred_element_type=jnp.float32
        )
        delta = jnp.sum(probs[None] * grad_probs, axis=(4, 5), keepdims=True)
        grad_scores = (probs[None] * (grad_probs - delta)).astype(jnp.bfloat16)
        query_terms = (
            softmax_scale
            * jnp.einsum(
                "rghqtk,gtkhd->rgqhd", grad_scores, key_tiles, preferred_element_type=jnp.float32
            )
        ).astype(jnp.bfloat16)
        key_terms = softmax_scale * jnp.einsum(
            "rghqtk,gqhd->rgtkhd", grad_scores, query_group, preferred_element_type=jnp.float32
        )
        value_terms = jnp.einsum(
            "ghqtk,rgqhd->rgtkhd", probs_bf, cot_group, preferred_element_type=jnp.float32
        )
        grad_keys = add_tiles(grad_keys, key_terms, onehot)
        grad_values = add_tiles(grad_values, value_terms, onehot)
        grad_query = lax.dynamic_update_slice_in_dim(grad_query, query_terms, offset_at, 1)
        return ((grad_query, grad_keys, grad_values), None)

    zeros_full = jnp.zeros((row_count,) + block_shape, jnp.float32)
    initial = (jnp.zeros((row_count,) + block_shape, jnp.bfloat16), zeros_full, zeros_full)
    finals, unused = lax.scan(step, initial, jnp.arange(block_count // group, dtype=jnp.int32))
    grad_query, grad_keys, grad_values = finals
    flat_shape = (row_count, seq_len, width_local)
    return (
        lax.all_to_all(
            grad_query.reshape(flat_shape), "seq", split_axis=1, concat_axis=2, tiled=True
        ),
        lax.all_to_all(
            grad_keys.reshape(flat_shape).astype(jnp.bfloat16),
            "seq",
            split_axis=1,
            concat_axis=2,
            tiled=True,
        ),
        lax.all_to_all(
            grad_values.reshape(flat_shape).astype(jnp.bfloat16),
            "seq",
            split_axis=1,
            concat_axis=2,
            tiled=True,
        ),
    )


def solution(mesh):
    placed = (
        P("seq", None),
        P("seq", None),
        P("seq", None),
        P("rows", "seq", None),
        P(),
        P("rows"),
        P("rows"),
        P(),
        P(),
    )
    return jax.shard_map(
        per_device,
        mesh=mesh,
        in_specs=placed,
        out_specs=(P("rows", "seq", None), P("rows", "seq", None), P("rows", "seq", None)),
        check_vma=False,
    )
```

profile of v0, /device:TPU:2, one launch (start us, length us, event | category | flops | bytes accessed | tf_op | source)
XLA Modules:
  0.0 763.2 jit_solution(254725159032341387)
XLA Ops:
  4.5 7.3 copy.236
  12.3 21.6 %reduce.1 = bf16[4096,256]{1,0:T(8,128)(2,1)S(1)} reduce(bf16[4096,1,256]{2,1,0:T(2,128)(2,1)} %bitcast.296, bf16[]{:T(256)} %broadcast.138), dimensions={1}, to_apply=%bitcast.195.reduce_sub_computation | reduce | bytes 4194306
  35.9 7.5 all-to-all-start.3
  43.4 4.1 copy.228
  47.4 23.1 %all-to-all-done.3 = bf16[16,2,32768]{2,1,0:T(2,128)(2,1)S(1)} async-done(((bf16[16,2,32768]{2,1,0:T(2,128)(2,1)}), bf16[16,2,32768]{2,1,0:T(2,128)(2,1)S(1)}, u32[]{:S(2)}, u32[]{:S(2)}) %all-to-all-start.3) | async-done | bytes 2097184 | tf_op jit(solution)/shard_map/all_to_all | solution.py:99
  70.5 7.5 all-to-all-start.1
  78.1 4.1 copy.226
  82.1 21.1 %all-to-all-done.1 = bf16[256,16,256]{0,2,1:T(8,128)(2,1)} async-done(((bf16[256,16,256]{0,2,1:T(8,128)(2,1)}), bf16[256,16,256]{0,2,1:T(8,128)(2,1)}, u32[]{:S(2)}, u32[]{:S(2)}) %all-to-all-start.1) | async-done | bytes 2097184 | tf_op jit(solution)/shard_map/all_to_all | solution.py:94
  103.2 7.1 all-to-all-start
  110.3 4.1 copy.234
  114.4 21.0 %all-to-all-done = bf16[256,16,256]{0,2,1:T(8,128)(2,1)} async-done(((bf16[256,16,256]{0,2,1:T(8,128)(2,1)}), bf16[256,16,256]{0,2,1:T(8,128)(2,1)}, u32[]{:S(2)}, u32[]{:S(2)}) %all-to-all-start) | async-done | bytes 2097184 | tf_op jit(solution)/shard_map/all_to_all | solution.py:95
  135.4 7.7 %all-to-all-start.2 = ((bf16[256,16,256]{0,2,1:T(8,128)(2,1)}), bf16[256,16,256]{0,2,1:T(8,128)(2,1)}, u32[]{:S(2)}, u32[]{:S(2)}) async-start(bf16[256,16,256]{0,2,1:T(8,128)(2,1)} %bitcast.309), calls=%async_computation.2 | async-start | bytes 4194304 | tf_op jit(solution)/shard_map/all_to_all | solution.py:96
  143.5 6.7 reshape.258
  161.0 4.3 copy.240
  170.2 5.1 copy.239
  178.2 4.1 copy.235
  182.3 4.1 reshape.226
  186.4 5.1 copy.241
  194.2 14.1 %all_gather.3 = f32[32,2,128]{2,1,0:T(2,128)S(1)} all-gather(f32[4,2,128]{2,1,0:T(2,128)S(1)} %bitcast.317), channel_id=1, replica_groups=mesh['rows'=8,'seq'=16] {'rows'}, dimensions={0}, use_global_device_ids=true | all-gather | bytes 36864 | tf_op jit(solution)/shard_map/all_gather | solution.py:120
  208.3 3.2 broadcast_in_dim.71.clone
  211.5 353.2 %while.5 = (s32[]{:T(128)}, bf16[1,32,128,2,128]{4,3,2,1,0:T(2,128)(2,1)}, f32[1,32,128,2,128]{4,1,3,2,0:T(8,128)}, f32[1,32,128,2,128]{4,1,3,2,0:T(8,128)}, s32...) while((s32[]{:T(128)}, ...), condition=%wide.region_4.5_spmd.clone, body=%wide.region_2.0_spmd.clone.sunk | while | flops 1784943616 | bytes 221541968 | solution.py:161
  256.4 3.5 copy.333
  280.7 3.1 fusion.164
  299.0 3.5 copy.333
  341.6 3.5 copy.333
  384.2 3.5 copy.333
  426.8 3.5 copy.333
  469.4 3.5 copy.333
  512.0 3.5 copy.333
  554.6 3.5 copy.333
  569.7 6.2 reshape.256
  575.9 21.6 %reduce.4 = bf16[4096,256]{1,0:T(8,128)(2,1)S(1)} reduce(bf16[4096,1,256]{2,1,0:T(2,128)(2,1)} %bitcast.299, bf16[]{:T(256)} %broadcast.138), dimensions={1}, to_apply=%bitcast.201.reduce_sub_computation | reduce | bytes 4194306
  599.5 7.3 all-to-all-start.6
  609.5 3.5 copy.270
  613.0 13.5 %reshape.255 = bf16[1,4096,256]{2,0,1:T(2,128)(2,1)} reshape(bf16[1,32,128,2,128]{4,3,2,1,0:T(2,128)(2,1)} %copy.270) | data formatting | bytes 4194304 | tf_op jit(solution)/shard_map/convert_element_type | solution.py:169
  626.5 22.9 %reduce.3 = bf16[4096,256]{1,0:T(8,128)(2,1)} reduce(bf16[4096,1,256]{2,1,0:T(2,128)(2,1)} %bitcast.300, bf16[]{:T(256)} %broadcast.138), dimensions={1}, to_apply=%bitcast.199.reduce_sub_computation | reduce | bytes 4194306
  649.4 3.9 reshape.261
  653.3 7.5 all-to-all-start.5
  660.9 13.5 %reshape.254 = bf16[1,4096,256]{2,0,1:T(2,128)(2,1)} reshape(bf16[1,32,128,2,128]{4,3,2,1,0:T(2,128)(2,1)} %get-tuple-element.88) | data formatting | bytes 4194304 | tf_op jit(solution)/shard_map/reshape | solution.py:166
  674.4 22.9 %reduce.2 = bf16[4096,256]{1,0:T(8,128)(2,1)} reduce(bf16[4096,1,256]{2,1,0:T(2,128)(2,1)} %bitcast.297, bf16[]{:T(256)} %broadcast.138), dimensions={1}, to_apply=%bitcast.197.reduce_sub_computation | reduce | bytes 4194306
  697.3 3.9 reshape.259
  701.2 7.2 all-to-all-start.4
  708.5 6.7 reshape.264
  720.1 4.1 copy.254
  724.1 10.4 %reshape.262 = bf16[4096,1,256]{2,1,0:T(2,128)(2,1)} reshape(bf16[16,2,32768]{2,1,0:T(2,128)(2,1)} %all-to-all-done.5) | data formatting | bytes 4194304
  739.5 4.1 copy.253
  743.5 10.4 %reshape.260 = bf16[4096,1,256]{2,1,0:T(2,128)(2,1)} reshape(bf16[16,2,32768]{2,1,0:T(2,128)(2,1)} %all-to-all-done.4) | data formatting | bytes 4194304
  758.9 4.1 copy.252
  (342 shorter events, 354.4 us)
Async XLA Ops:
  35.9 34.6 %all-to-all-start.3 = ((bf16[16,2,32768]{2,1,0:T(2,128)(2,1)}), bf16[16,2,32768]{2,1,0:T(2,128)(2,1)S(1)}, u32[]{:S(2)}, u32[]{:S(2)}) async-start(bf16[16,2,32768]{2,1,0:T(2,128)(2,1)} %reshape.257), calls=%async_computation.3 | async-start | bytes 4194304 | tf_op jit(solution)/shard_map/all_to_all | solution.py:99
  70.5 32.7 %all-to-all-start.1 = ((bf16[256,16,256]{0,2,1:T(8,128)(2,1)}), bf16[256,16,256]{0,2,1:T(8,128)(2,1)}, u32[]{:S(2)}, u32[]{:S(2)}) async-start(bf16[256,16,256]{0,2,1:T(8,128)(2,1)} %bitcast.310), calls=%async_computation.1 | async-start | bytes 4194304 | tf_op jit(solution)/shard_map/all_to_all | solution.py:94
  103.2 32.2 %all-to-all-start = ((bf16[256,16,256]{0,2,1:T(8,128)(2,1)}), bf16[256,16,256]{0,2,1:T(8,128)(2,1)}, u32[]{:S(2)}, u32[]{:S(2)}) async-start(bf16[256,16,256]{0,2,1:T(8,128)(2,1)} %bitcast.311), calls=%async_computation | async-start | bytes 4194304 | tf_op jit(solution)/shard_map/all_to_all | solution.py:95
  135.4 7.8 %copy-start.7 = (s32[32,8]{0,1:T(8,128)S(1)}, s32[32,8]{0,1:T(8,128)}, u32[]{:S(2)}) copy-start(s32[32,8]{0,1:T(8,128)} %param.18) | copy-start | bytes 3076
  135.4 7.8 %copy-start.8 = (s32[32]{0:T(128)S(1)}, s32[32]{0:T(128)}, u32[]{:S(2)}) copy-start(s32[32]{0:T(128)} %param.19) | copy-start | bytes 388
  135.4 42.8 %all-to-all-start.2 = ((bf16[256,16,256]{0,2,1:T(8,128)(2,1)}), bf16[256,16,256]{0,2,1:T(8,128)(2,1)}, u32[]{:S(2)}, u32[]{:S(2)}) async-start(bf16[256,16,256]{0,2,1:T(8,128)(2,1)} %bitcast.309), calls=%async_computation.2 | async-start | bytes 4194304 | tf_op jit(solution)/shard_map/all_to_all | solution.py:96
  245.3 2.2 copy-start.5
  247.5 2.9 copy-start.2
  250.4 2.6 copy-start.6
  259.9 2.8 copy-start.3
  264.1 2.0 copy-start.4
  287.9 2.2 copy-start.5
  290.1 2.9 copy-start.2
  293.0 2.6 copy-start.6
  302.5 2.8 copy-start.3
  330.5 2.2 copy-start.5
  332.7 2.9 copy-start.2
  335.6 2.6 copy-start.6
  345.1 2.8 copy-start.3
  349.3 2.0 copy-start.4
  373.1 2.2 copy-start.5
  375.3 2.9 copy-start.2
  378.2 2.6 copy-start.6
  387.7 2.8 copy-start.3
  391.9 2.0 copy-start.4
  415.7 2.2 copy-start.5
  417.9 2.9 copy-start.2
  420.8 2.6 copy-start.6
  430.3 2.8 copy-start.3
  434.5 2.0 copy-start.4
  458.3 2.2 copy-start.5
  460.5 2.9 copy-start.2
  463.4 2.6 copy-start.6
  472.9 2.8 copy-start.3
  500.9 2.2 copy-start.5
  503.1 2.9 copy-start.2
  506.0 2.6 copy-start.6
  515.5 2.8 copy-start.3
  519.7 2.0 copy-start.4
  543.5 2.2 copy-start.5
  545.7 2.9 copy-start.2
  548.6 2.6 copy-start.6
  558.1 2.8 copy-start.3
  562.3 2.0 copy-start.4
  599.5 53.9 %all-to-all-start.6 = ((bf16[16,2,32768]{2,1,0:T(2,128)(2,1)}), bf16[16,2,32768]{2,1,0:T(2,128)(2,1)S(1)}, u32[]{:S(2)}, u32[]{:S(2)}) async-start(bf16[16,2,32768]{2,1,0:T(2,128)(2,1)} %reshape.263), calls=%async_computation.6 | async-start | bytes 4194304 | tf_op jit(solution)/shard_map/all_to_all | solution.py:175
  653.3 47.9 %all-to-all-start.5 = ((bf16[16,2,32768]{2,1,0:T(2,128)(2,1)}), bf16[16,2,32768]{2,1,0:T(2,128)(2,1)}, u32[]{:S(2)}, u32[]{:S(2)}) async-start(bf16[16,2,32768]{2,1,0:T(2,128)(2,1)} %reshape.261), calls=%async_computation.5 | async-start | bytes 4194304 | tf_op jit(solution)/shard_map/all_to_all | solution.py:168
  701.2 42.3 %all-to-all-start.4 = ((bf16[16,2,32768]{2,1,0:T(2,128)(2,1)}), bf16[16,2,32768]{2,1,0:T(2,128)(2,1)}, u32[]{:S(2)}, u32[]{:S(2)}) async-start(bf16[16,2,32768]{2,1,0:T(2,128)(2,1)} %reshape.259), calls=%async_computation.4 | async-start | bytes 4194304 | tf_op jit(solution)/shard_map/all_to_all | solution.py:165
  758.9 4.1 copy-start.1
  (3 other events, 5.3 us)
where the time goes:
time: 773 us; the launch traced here: 763 us
  local copies, waits for them, and re-layouts  281 us (36%)
  matrix products  188 us (24%)
  other arithmetic  142 us (18%)
  waiting for transfers between devices  65.2 us (8%)
  starting transfers between devices  51.9 us (7%)
  loops' own time  18.8 us (2%)
  blocking collectives  14.1 us (2%)
    unnamed x31, local copies, waits for them, and re-layouts  95.8 us
    unnamed x6, other arithmetic  88.9 us
    another operation x16, local copies, waits for them, and re-layouts  52.3 us
    another operation x40, other arithmetic  43.5 us
    dot_general x17, matrix products, pick_tiles(): jnp.einsum('gtb,bkhd->gtkhd', onehot, blocks, preferred_element_type=jnp....  39.9 us
    dot_general x16, matrix products, add_tiles(): jnp.einsum('gtb,rgtkhd->rbkhd', onehot, low_part, preferred_element_type=...  34.5 us
    dot_general x16, matrix products, add_tiles(): jnp.einsum('gtb,rgtkhd->rbkhd', onehot, high_part, preferred_element_type...  33.9 us
    dot_general x8, matrix products, step(): jnp.einsum('ghqtk,rgqhd->rgtkhd', probs_bf, cot_group, preferred_element_...  25.2 us
  transfers between devices with their start and end apart: 7, of which 3 were waited for; matrix products, arithmetic and copies ran while one was open for 22% of the time, Pallas kernels for 0%

commit v1 on v0

--- a/solution.py
+++ b/solution.py
@@ -96,7 +96,10 @@
         lax.all_to_all(values, "seq", split_axis=1, concat_axis=0, tiled=True),
     )
     cotangent = substitute(grad_out, table, positions, residues, lax.axis_index("seq") * tok_count)
-    cot_heads = lax.all_to_all(cotangent, "seq", split_axis=2, concat_axis=1, tiled=True)
+    cot_heads = jnp.concatenate(
+        lax.all_to_all(jnp.stack(jnp.split(cotangent, lax.axis_size("seq"), axis=2)), "seq", 0, 0),
+        axis=1,
+    )
     seq_len = query_heads.shape[0]
     width_local = query_heads.shape[1]
     heads_local = width_local // D_HEAD

time: 773 us -> 718 us (0.929)
  other arithmetic: 142 us -> 120 us
  loops' own time: 18.8 us -> 6.85 us
  waiting for transfers between devices: 65.2 us -> 54.8 us
  local copies, waits for them, and re-layouts: 281 us -> 272 us
    all_to_all x1, waiting for transfers between devices: 23.1 us -> 0.01 us  [per_device(): lax.all_to_all(jnp.stack(jnp.split(cotangent, lax.axis_size('seq'), axis=...]
    unnamed x6 -> x5, other arithmetic: 88.9 us -> 67.5 us
    all_to_all x1, waiting for transfers between devices: 0.01 us -> 19.1 us  [per_device(): lax.all_to_all(values, 'seq', split_axis=1, concat_axis=0, tiled=True)]
    another operation x1, loops' own time: 18.8 us -> 6.85 us  [per_device(): lax.scan(step, initial, jnp.arange(block_count // group, dtype=jnp.int32))]
    another operation x16 -> x18, local copies, waits for them, and re-layouts: 52.3 us -> 56.6 us
    unnamed x31 -> x47, local copies, waits for them, and re-layouts: 95.8 us -> 94.7 us
  transfers between devices with their start and end apart: 7 -> 7, of which waited for: 3 -> 3; matrix products, arithmetic and copies ran while one was open for 22% -> 25% of each run, Pallas kernels for 0% -> 0%
where the time goes in v1:
time: 718 us; the launch traced here: 710 us
  local copies, waits for them, and re-layouts  272 us (38%)
  matrix products  188 us (26%)
  other arithmetic  120 us (17%)
  waiting for transfers between devices  54.8 us (8%)
  starting transfers between devices  51.9 us (7%)
  blocking collectives  14.1 us (2%)
    unnamed x47, local copies, waits for them, and re-layouts  94.7 us
    unnamed x5, other arithmetic  67.5 us
    another operation x16, local copies, waits for them, and re-layouts  52 us
    another operation x40, other arithmetic  43.3 us
    dot_general x17, matrix products, pick_tiles(): jnp.einsum('gtb,bkhd->gtkhd', onehot, blocks, preferred_element_type=jnp....  39.7 us
    dot_general x16, matrix products, add_tiles(): jnp.einsum('gtb,rgtkhd->rbkhd', onehot, low_part, preferred_element_type=...  34.5 us
    dot_general x16, matrix products, add_tiles(): jnp.einsum('gtb,rgtkhd->rbkhd', onehot, high_part, preferred_element_type...  33.8 us
    dot_general x8, matrix products, step(): jnp.einsum('ghqtk,rgqhd->rgtkhd', probs_bf, cot_group, preferred_element_...  25 us
  transfers between devices with their start and end apart: 7, of which 3 were waited for; matrix products, arithmetic and copies ran while one was open for 25% of the time, Pallas kernels for 0%

profile of v1, /device:TPU:2, one launch (start us, length us, event | category | flops | bytes accessed | tf_op | source)
XLA Modules:
  0.0 709.6 jit_solution(17822086281596393366)
XLA Ops:
  0.6 4.1 copy.144
  4.8 7.5 %all-to-all-start.1 = ((bf16[256,16,256]{0,2,1:T(8,128)(2,1)}), bf16[256,16,256]{0,2,1:T(8,128)(2,1)S(1)}, u32[]{:S(2)}, u32[]{:S(2)}) async-start(bf16[256,16,256]{0,2,1:T(8,128)(2,1)} %bitcast.365), calls=%async_computation.1 | async-start | bytes 4194304 | tf_op jit(solution)/shard_map/all_to_all | solution.py:94
  13.5 4.1 copy.142
  17.8 21.6 %all-to-all-done.1 = bf16[256,16,256]{0,2,1:T(8,128)(2,1)S(1)} async-done(((bf16[256,16,256]{0,2,1:T(8,128)(2,1)}), bf16[256,16,256]{0,2,1:T(8,128)(2,1)S(1)}, u32[]{:S(2)}, u32[]{:S(2)}) %all-to-all-start.1) | async-done | bytes 2097184 | tf_op jit(solution)/shard_map/all_to_all | solution.py:94
  40.7 7.5 %all-to-all-start = ((bf16[256,16,256]{0,2,1:T(8,128)(2,1)}), bf16[256,16,256]{0,2,1:T(8,128)(2,1)}, u32[]{:S(2)}, u32[]{:S(2)}) async-start(bf16[256,16,256]{0,2,1:T(8,128)(2,1)} %bitcast.364), calls=%async_computation | async-start | bytes 4194304 | tf_op jit(solution)/shard_map/all_to_all | solution.py:95
  50.5 4.1 copy.150
  59.3 14.1 %all-to-all-done = bf16[256,16,256]{0,2,1:T(8,128)(2,1)} async-done(((bf16[256,16,256]{0,2,1:T(8,128)(2,1)}), bf16[256,16,256]{0,2,1:T(8,128)(2,1)}, u32[]{:S(2)}, u32[]{:S(2)}) %all-to-all-start) | async-done | bytes 2097184 | tf_op jit(solution)/shard_map/all_to_all | solution.py:95
  73.4 7.1 all-to-all-start.2
  86.5 19.1 %all-to-all-done.2 = bf16[256,16,256]{0,2,1:T(8,128)(2,1)} async-done(((bf16[256,16,256]{0,2,1:T(8,128)(2,1)}), bf16[256,16,256]{0,2,1:T(8,128)(2,1)}, u32[]{:S(2)}, u32[]{:S(2)}) %all-to-all-start.2) | async-done | bytes 2097184 | tf_op jit(solution)/shard_map/all_to_all | solution.py:96
  105.6 7.8 %all-to-all-start.3 = ((bf16[16,1,256,256]{3,2,1,0:T(8,128)(2,1)}), bf16[16,1,256,256]{3,2,1,0:T(8,128)(2,1)}, u32[]{:S(2)}, u32[]{:S(2)}) async-start(bf16[16,1,256,256]{3,2,1,0:T(8,128)(2,1)} %fusion.83), calls=%async_computation.3 | async-start | bytes 4194304 | tf_op jit(solution)/shard_map/all_to_all | solution.py:100
  126.6 5.1 copy.154
  134.6 4.1 copy.151
  138.6 4.1 reshape.222
  142.7 5.1 copy.156
  150.5 14.1 %all_gather.3 = f32[32,2,128]{2,1,0:T(2,128)S(1)} all-gather(f32[4,2,128]{2,1,0:T(2,128)S(1)} %bitcast.371), channel_id=1, replica_groups=mesh['rows'=8,'seq'=16] {'rows'}, dimensions={0}, use_global_device_ids=true | all-gather | bytes 36864 | tf_op jit(solution)/shard_map/all_gather | solution.py:123
  164.6 4.0 reshape.249
  168.6 3.2 broadcast_in_dim.71.clone
  171.8 338.4 %while.5 = (s32[]{:T(128)}, bf16[1,32,128,2,128]{4,3,2,1,0:T(2,128)(2,1)}, f32[1,32,128,2,128]{4,1,3,2,0:T(8,128)}, f32[1,32,128,2,128]{4,1,3,2,0:T(8,128)}, s32...) while((s32[]{:T(128)}, ...), condition=%wide.region_4.5_spmd.clone, body=%wide.region_2.0_spmd.clone.sunk | while | flops 1784943616 | bytes 221017680 | solution.py:164
  186.2 3.1 fusion.176
  204.5 3.5 copy.256
  246.8 3.5 copy.256
  270.7 3.1 fusion.176
  289.0 3.5 copy.256
  312.9 3.1 fusion.176
  331.2 3.5 copy.256
  355.2 3.1 fusion.176
  373.4 3.5 copy.256
  415.6 3.5 copy.256
  457.9 3.5 copy.256
  500.1 3.5 copy.256
  515.2 6.2 reshape.252
  522.0 21.6 %reduce.3 = bf16[4096,256]{1,0:T(8,128)(2,1)S(1)} reduce(bf16[4096,1,256]{2,1,0:T(2,128)(2,1)} %bitcast.352, bf16[]{:T(256)} %broadcast.138), dimensions={1}, to_apply=%bitcast.257.reduce_sub_computation | reduce | bytes 4194306
  545.6 7.3 %all-to-all-start.6 = ((bf16[16,2,32768]{2,1,0:T(2,128)(2,1)}), bf16[16,2,32768]{2,1,0:T(2,128)(2,1)S(1)}, u32[]{:S(2)}, u32[]{:S(2)}) async-start(bf16[16,2,32768]{2,1,0:T(2,128)(2,1)} %reshape.257), calls=%async_computation.6 | async-start | bytes 4194304 | tf_op jit(solution)/shard_map/all_to_all | solution.py:178
  555.6 3.5 copy.187
  559.1 13.5 %reshape.251 = bf16[1,4096,256]{2,0,1:T(2,128)(2,1)} reshape(bf16[1,32,128,2,128]{4,3,2,1,0:T(2,128)(2,1)} %copy.187) | data formatting | bytes 4194304 | tf_op jit(solution)/shard_map/convert_element_type | solution.py:172
  572.6 22.9 %reduce.2 = bf16[4096,256]{1,0:T(8,128)(2,1)} reduce(bf16[4096,1,256]{2,1,0:T(2,128)(2,1)} %bitcast.354, bf16[]{:T(256)} %broadcast.138), dimensions={1}, to_apply=%bitcast.255.reduce_sub_computation | reduce | bytes 4194306
  595.5 4.0 reshape.255
  599.5 7.5 %all-to-all-start.5 = ((bf16[16,2,32768]{2,1,0:T(2,128)(2,1)}), bf16[16,2,32768]{2,1,0:T(2,128)(2,1)}, u32[]{:S(2)}, u32[]{:S(2)}) async-start(bf16[16,2,32768]{2,1,0:T(2,128)(2,1)} %reshape.255), calls=%async_computation.5 | async-start | bytes 4194304 | tf_op jit(solution)/shard_map/all_to_all | solution.py:171
  607.1 13.5 %reshape.250 = bf16[1,4096,256]{2,0,1:T(2,128)(2,1)} reshape(bf16[1,32,128,2,128]{4,3,2,1,0:T(2,128)(2,1)} %get-tuple-element.88) | data formatting | bytes 4194304 | tf_op jit(solution)/shard_map/reshape | solution.py:169
  620.6 22.9 %reduce.1 = bf16[4096,256]{1,0:T(8,128)(2,1)} reduce(bf16[4096,1,256]{2,1,0:T(2,128)(2,1)} %bitcast.353, bf16[]{:T(256)} %broadcast.138), dimensions={1}, to_apply=%bitcast.253.reduce_sub_computation | reduce | bytes 4194306
  643.5 3.9 reshape.253
  647.5 7.2 %all-to-all-start.4 = ((bf16[16,2,32768]{2,1,0:T(2,128)(2,1)}), bf16[16,2,32768]{2,1,0:T(2,128)(2,1)}, u32[]{:S(2)}, u32[]{:S(2)}) async-start(bf16[16,2,32768]{2,1,0:T(2,128)(2,1)} %reshape.253), calls=%async_computation.4 | async-start | bytes 4194304 | tf_op jit(solution)/shard_map/all_to_all | solution.py:168
  654.7 6.8 reshape.258
  666.4 4.1 copy.169
  670.5 10.5 %reshape.256 = bf16[4096,1,256]{2,1,0:T(2,128)(2,1)} reshape(bf16[16,2,32768]{2,1,0:T(2,128)(2,1)} %all-to-all-done.5) | data formatting | bytes 4194304
  685.9 4.1 copy.168
  690.0 10.5 %reshape.254 = bf16[4096,1,256]{2,1,0:T(2,128)(2,1)} reshape(bf16[16,2,32768]{2,1,0:T(2,128)(2,1)} %all-to-all-done.4) | data formatting | bytes 4194304
  705.3 4.1 copy.167
  (348 shorter events, 349.2 us)
Async XLA Ops:
  0.6 17.0 %copy-start = (bf16[33,4096]{1,0:T(8,128)(2,1)S(1)}, bf16[33,4096]{1,0:T(8,128)(2,1)}, u32[]{:S(2)}) copy-start(bf16[33,4096]{1,0:T(8,128)(2,1)} %param.15) | copy-start | bytes 811012
  4.8 34.6 %all-to-all-start.1 = ((bf16[256,16,256]{0,2,1:T(8,128)(2,1)}), bf16[256,16,256]{0,2,1:T(8,128)(2,1)S(1)}, u32[]{:S(2)}, u32[]{:S(2)}) async-start(bf16[256,16,256]{0,2,1:T(8,128)(2,1)} %bitcast.365), calls=%async_computation.1 | async-start | bytes 4194304 | tf_op jit(solution)/shard_map/all_to_all | solution.py:94
  40.7 32.7 %all-to-all-start = ((bf16[256,16,256]{0,2,1:T(8,128)(2,1)}), bf16[256,16,256]{0,2,1:T(8,128)(2,1)}, u32[]{:S(2)}, u32[]{:S(2)}) async-start(bf16[256,16,256]{0,2,1:T(8,128)(2,1)} %bitcast.364), calls=%async_computation | async-start | bytes 4194304 | tf_op jit(solution)/shard_map/all_to_all | solution.py:95
  73.4 32.2 %all-to-all-start.2 = ((bf16[256,16,256]{0,2,1:T(8,128)(2,1)}), bf16[256,16,256]{0,2,1:T(8,128)(2,1)}, u32[]{:S(2)}, u32[]{:S(2)}) async-start(bf16[256,16,256]{0,2,1:T(8,128)(2,1)} %bitcast.363), calls=%async_computation.2 | async-start | bytes 4194304 | tf_op jit(solution)/shard_map/all_to_all | solution.py:96
  86.5 26.9 %copy-start.9 = (s32[32,8]{0,1:T(8,128)S(1)}, s32[32,8]{0,1:T(8,128)}, u32[]{:S(2)}) copy-start(s32[32,8]{0,1:T(8,128)} %param.18) | copy-start | bytes 3076
  86.5 26.9 %copy-start.10 = (s32[32]{0:T(128)S(1)}, s32[32]{0:T(128)}, u32[]{:S(2)}) copy-start(s32[32]{0:T(128)} %param.19) | copy-start | bytes 388
  86.5 27.2 %copy-start.8 = (bf16[256,16,256]{0,2,1:T(8,128)(2,1)S(1)}, bf16[256,16,256]{0,2,1:T(8,128)(2,1)}, u32[]{:S(2)}) copy-start(bf16[256,16,256]{0,2,1:T(8,128)(2,1)} %copy-done.7) | copy-start | bytes 6291460
  105.6 59.0 %all-to-all-start.3 = ((bf16[16,1,256,256]{3,2,1,0:T(8,128)(2,1)}), bf16[16,1,256,256]{3,2,1,0:T(8,128)(2,1)}, u32[]{:S(2)}, u32[]{:S(2)}) async-start(bf16[16,1,256,256]{3,2,1,0:T(8,128)(2,1)} %fusion.83), calls=%async_computation.3 | async-start | bytes 4194304 | tf_op jit(solution)/shard_map/all_to_all | solution.py:100
  193.4 2.2 copy-start.5
  195.6 2.9 copy-start.2
  198.5 2.6 copy-start.6
  208.0 2.8 copy-start.3
  212.2 2.0 copy-start.4
  235.6 2.2 copy-start.5
  237.8 2.9 copy-start.2
  240.8 2.6 copy-start.6
  250.3 2.8 copy-start.3
  254.5 2.0 copy-start.4
  277.9 2.2 copy-start.5
  280.1 2.9 copy-start.2
  283.0 2.6 copy-start.6
  292.5 2.8 copy-start.3
  296.7 2.0 copy-start.4
  320.1 2.2 copy-start.5
  322.3 2.9 copy-start.2
  325.2 2.6 copy-start.6
  334.7 2.8 copy-start.3
  338.9 2.0 copy-start.4
  362.3 2.2 copy-start.5
  364.5 2.9 copy-start.2
  367.4 2.6 copy-start.6
  376.9 2.8 copy-start.3
  404.5 2.2 copy-start.5
  406.7 2.9 copy-start.2
  409.7 2.6 copy-start.6
  419.2 2.8 copy-start.3
  446.8 2.2 copy-start.5
  448.9 2.9 copy-start.2
  451.9 2.6 copy-start.6
  461.4 2.8 copy-start.3
  489.0 2.2 copy-start.5
  491.2 2.9 copy-start.2
  494.1 2.6 copy-start.6
  503.6 2.8 copy-start.3
  545.6 53.9 %all-to-all-start.6 = ((bf16[16,2,32768]{2,1,0:T(2,128)(2,1)}), bf16[16,2,32768]{2,1,0:T(2,128)(2,1)S(1)}, u32[]{:S(2)}, u32[]{:S(2)}) async-start(bf16[16,2,32768]{2,1,0:T(2,128)(2,1)} %reshape.257), calls=%async_computation.6 | async-start | bytes 4194304 | tf_op jit(solution)/shard_map/all_to_all | solution.py:178
  599.5 48.0 %all-to-all-start.5 = ((bf16[16,2,32768]{2,1,0:T(2,128)(2,1)}), bf16[16,2,32768]{2,1,0:T(2,128)(2,1)}, u32[]{:S(2)}, u32[]{:S(2)}) async-start(bf16[16,2,32768]{2,1,0:T(2,128)(2,1)} %reshape.255), calls=%async_computation.5 | async-start | bytes 4194304 | tf_op jit(solution)/shard_map/all_to_all | solution.py:171
  647.5 42.5 %all-to-all-start.4 = ((bf16[16,2,32768]{2,1,0:T(2,128)(2,1)}), bf16[16,2,32768]{2,1,0:T(2,128)(2,1)}, u32[]{:S(2)}, u32[]{:S(2)}) async-start(bf16[16,2,32768]{2,1,0:T(2,128)(2,1)} %reshape.253), calls=%async_computation.4 | async-start | bytes 4194304 | tf_op jit(solution)/shard_map/all_to_all | solution.py:168
  705.3 4.1 copy-start.1
  (5 other events, 9.2 us)
